TPU v7x, 32 devices: a whole 2x2x4 slice. The times are simulated.
32 devices in a mesh: ctx: 8 (over y, x, core), tp: 4 (over z).
Axes of the slice: x: 2, y: 2, z: 4, core: 2. Of those that a mesh axis runs over, the one named last changes fastest.
Arguments:
- inputs: bfloat16 [4096, 2048], P(('ctx', 'tp')), may hold values from -54 to 54
- norm_gain: float32 [2048], replicated, may hold values from 0.1 to 1.9
- qkv_weight: bfloat16 [2048, 3, 2048], P(None, None, 'tp'), may hold values from -0.125 to 0.125
- head_gain: float32 [2048], P('tp'), may hold values from 0.1 to 1.9
- out_weight: bfloat16 [2048, 2048], P('tp'), may hold values from -0.125 to 0.125
- out_cotangent: bfloat16 [4096, 2048], P(('ctx', 'tp')), may hold values from -6 to 6
Outputs:
- outputs: bfloat16 [4096, 2048], P(('ctx', 'tp'))
- input_grad: bfloat16 [4096, 2048], P(('ctx', 'tp'))
- qkv_grad: float32 [2048, 3, 2048], P('ctx', None, 'tp')
- out_grad_t: float32 [2048, 2048], P('ctx', 'tp')
All inputs are finite; a program needn't handle non-finite values.
Results may differ from a plain program's by a relative error of at most 0.015.
The roundings to bfloat16 on the way count: a program that leaves them out, or rounds other values in their place, can miss the bound.
Values may be sent and summed in bfloat16 or wider, within the bound.
A program may use at most 128 MiB of HBM per device.

v0:
```python
import math

import jax
import jax.numpy as jnp
from jax import lax
from jax.sharding import PartitionSpec as P

DH = 128


EPSILON = 1e-05
highest = lax.Precision.HIGHEST


def carried_in(array, axis, combine, identity, reverse):
    devices, place = (lax.axis_size(axis), lax.axis_index(axis))
    everything = lax.all_gather(array.astype(jnp.bfloat16), axis)
    start = jnp.broadcast_to(jnp.asarray(identity, array.dtype), array.shape)

    def hop(k, before):
        at = devices - 1 - k if reverse else k
        reached = at > place if reverse else at < place
        new = combine(before, everything[at].astype(array.dtype))
        return jnp.where(reached, new, before)

    return lax.fori_loop(0, devices, hop, start)


def row_scale(rows):
    return lax.rsqrt(jnp.mean(rows * rows, axis=-1, keepdims=True) + EPSILON)


def add_states(earlier, later):
    return earlier + later


def shards(inputs, norm_gain, qkv_weight, head_gain, out_weight, out_cotangent):
    width = inputs.shape[1]
    local_width = qkv_weight.shape[2]
    heads = local_width // DH
    own_rows = inputs.shape[0]
    block = own_rows * lax.axis_size("tp")
    total_tokens = block * lax.axis_size("ctx")
    factor = 1.0 / math.sqrt(total_tokens)
    ctx_rows = width // lax.axis_size("ctx")
    flat_weight = qkv_weight.reshape(width, 3 * local_width)
    piece_f = lax.all_gather(inputs, "tp", axis=0, tiled=True).astype(jnp.float32)
    normed_rows = (piece_f * row_scale(piece_f) * norm_gain).astype(jnp.bfloat16)
    projected_rows = jnp.dot(normed_rows, flat_weight, preferred_element_type=jnp.float32).astype(
        jnp.bfloat16
    )
    joined = jnp.concatenate([normed_rows, projected_rows], axis=1)
    normed = joined[:, :width]
    projected = joined[:, width:].reshape(block, 3, heads, DH)
    queries = projected[:, 0]
    key_rows = projected[:, 1]
    values = projected[:, 2]
    local_states = jnp.einsum("shd,she->hde", key_rows, values, preferred_element_type=jnp.float32)
    empty_states = jnp.zeros_like(local_states)
    states = carried_in(local_states, "ctx", add_states, empty_states, False)
    causal = jnp.arange(block)[:, None] >= jnp.arange(block)[None, :]
    raw_scores = jnp.einsum("thd,shd->hts", queries, key_rows, preferred_element_type=jnp.float32)
    scores = jnp.where(causal[None], raw_scores, 0.0).astype(jnp.bfloat16)
    local_part = jnp.einsum("hts,she->the", scores, values, preferred_element_type=jnp.float32)
    carried = jnp.einsum("thd,hde->the", queries.astype(jnp.float32), states, precision=highest)
    attended = local_part + carried
    scale_head = row_scale(attended)
    gains = head_gain.reshape(heads, DH)
    mixed = (attended * scale_head * gains).astype(jnp.bfloat16).reshape(block, local_width)
    rows = mixed
    attn_sum = lax.psum_scatter(
        jnp.dot(rows, out_weight, preferred_element_type=jnp.float32).astype(jnp.bfloat16),
        "tp",
        scatter_dimension=0,
        tiled=True,
    ).astype(jnp.float32)
    inputs_f = inputs.astype(jnp.float32)
    outputs = (inputs_f + attn_sum).astype(jnp.bfloat16)
    cotangent = lax.all_gather(out_cotangent, "tp", axis=0, tiled=True)
    grad_mixed = lax.dot_general(
        cotangent, out_weight, (((1,), (1,)), ((), ())), preferred_element_type=jnp.float32
    ).reshape(block, heads, DH)
    weighted = grad_mixed * gains
    cube_head = scale_head * scale_head * scale_head
    grad_attended = (
        scale_head * weighted
        - cube_head * attended * jnp.mean(weighted * attended, axis=-1, keepdims=True)
    ).astype(jnp.bfloat16)
    local_grads = jnp.einsum(
        "thd,the->hde", queries, grad_attended, preferred_element_type=jnp.float32
    )
    columns = cotangent
    out_grad_t = lax.psum_scatter(
        (
            lax.dot_general(
                columns, mixed, (((0,), (0,)), ((), ())), preferred_element_type=jnp.float32
            )
            * factor
        ).astype(jnp.bfloat16),
        "ctx",
        scatter_dimension=0,
        tiled=True,
    ).astype(jnp.float32)
    raw_grad = jnp.einsum("the,she->hts", grad_attended, values, preferred_element_type=jnp.float32)
    grad_scores = jnp.where(causal[None], raw_grad, 0.0).astype(jnp.bfloat16)
    grad_query = (
        jnp.einsum("hts,shd->thd", grad_scores, key_rows, preferred_element_type=jnp.float32)
        + jnp.einsum("the,hde->thd", grad_attended.astype(jnp.float32), states, precision=highest)
    ).astype(jnp.bfloat16)
    grad_states = carried_in(local_grads, "ctx", add_states, empty_states, True)
    grad_key = jnp.einsum(
        "hts,thd->shd", grad_scores, queries, preferred_element_type=jnp.float32
    ) + jnp.einsum("she,hde->shd", values.astype(jnp.float32), grad_states, precision=highest)
    grad_value = jnp.einsum(
        "hts,the->she", scores, grad_attended, preferred_element_type=jnp.float32
    ) + jnp.einsum("shd,hde->she", key_rows.astype(jnp.float32), grad_states, precision=highest)
    grad_key, grad_value = (grad_key.astype(jnp.bfloat16), grad_value.astype(jnp.bfloat16))
    grad_proj = jnp.stack([grad_query, grad_key, grad_value], axis=1).reshape(
        block, 3 * local_width
    )
    columns = normed
    product = lax.dot_general(
        columns, grad_proj, (((0,), (0,)), ((), ())), preferred_element_type=jnp.float32
    )
    qkv_grad = lax.psum_scatter(
        (product * factor)
        .reshape(ctx_rows * lax.axis_size("ctx"), 3, local_width)
        .astype(jnp.bfloat16),
        "ctx",
        scatter_dimension=0,
        tiled=True,
    ).astype(jnp.float32)
    rows = grad_proj
    grad_normed = lax.psum_scatter(
        lax.dot_general(
            rows, flat_weight, (((1,), (1,)), ((), ())), preferred_element_type=jnp.float32
        ).astype(jnp.bfloat16),
        "tp",
        scatter_dimension=0,
        tiled=True,
    ).astype(jnp.float32)
    scale_in = row_scale(inputs_f)
    weighted_in = grad_normed * norm_gain
    cube_in = scale_in * scale_in * scale_in
    input_grad = (
        out_cotangent.astype(jnp.float32)
        + scale_in * weighted_in
        - cube_in * inputs_f * jnp.mean(weighted_in * inputs_f, axis=-1, keepdims=True)
    ).astype(jnp.bfloat16)
    return (outputs, input_grad, qkv_grad, out_grad_t)


def solution(mesh):
    in_specs = (
        P(("ctx", "tp"), None),
        P(),
        P(None, None, "tp"),
        P("tp"),
        P("tp", None),
        P(("ctx", "tp"), None),
    )
    out_specs = (
        P(("ctx", "tp"), None),
        P(("ctx", "tp"), None),
        P("ctx", None, "tp"),
        P("ctx", "tp"),
    )
    return jax.shard_map(shards, mesh=mesh, in_specs=in_specs, out_specs=out_specs, check_vma=False)
```

profile of v0, /device:TPU:0, one launch (start us, length us, event | category | flops | bytes accessed | tf_op | source)
XLA Modules:
  0.0 377.1 jit_solution(10722562484087680778)
XLA Ops:
  8.7 8.8 %copy.45 = bf16[2048,3,512]{0,2,1:T(8,128)(2,1)} copy(bf16[2048,3,512]{2,0,1:T(8,128)(2,1)} %param.12) | data formatting | bytes 12582912 | tf_op args[2]
  17.6 40.7 %all-gather.7.cloned.1.call-done = bf16[512,2048]{1,0:T(8,128)(2,1)} async-done(((bf16[128,2048]{1,0:T(8,128)(2,1)}), bf16[512,2048]{1,0:T(8,128)(2,1)}) %all-gather.7.cloned.1.call-update) | async-done | bytes 2097168 | tf_op jit(solution)/shard_map/all_gather | solution.py:47
  60.5 7.6 %convolution_convert_fusion.2 = bf16[512,1536]{1,0:T(8,128)(2,1)} fusion(bf16[2048,1536]{0,1:T(8,128)(2,1)} %bitcast.80, bf16[512,2048]{1,0:T(8,128)(2,1)S(1)} %copy-done.12, f32[2048]{0:T(1024)S(1)} %copy-done.19, f32[512]{0:T(512)S(1)} %add_rsqrt_fusion.1), kind=kOutput, calls=%fused_computation.13 | convolution fusion | flops 3226206208 | bytes 9971712 | tf_op jit(solution)/shard_map/dot_general | solution.py:49
  68.1 3.9 %reshape.88 = bf16[512,3,4,128]{3,2,1,0:T(4,128)(2,1)} reshape(bf16[512,1536]{1,0:T(8,128)(2,1)} %convolution_convert_fusion.2) | data formatting | bytes 3145728 | tf_op jit(solution)/shard_map/reshape | solution.py:54
  72.1 2.9 fusion.26
  76.3 2.2 convolution_convert_fusion.4
  83.8 20.7 %all-gather.9.cloned.1.call-done = bf16[512,2048]{1,0:T(8,128)(2,1)} async-done(((bf16[128,2048]{1,0:T(8,128)(2,1)}), bf16[512,2048]{1,0:T(8,128)(2,1)}) %all-gather.9.cloned.1.call-update) | async-done | bytes 2097168 | tf_op jit(solution)/shard_map/all_gather | solution.py:79
  104.5 3.8 %fusion.27 = f32[512,512]{0,1:T(8,128)} fusion(bf16[512,2048]{1,0:T(8,128)(2,1)} %all-gather.9.cloned.1.call-done, bf16[512,2048]{1,0:T(8,128)(2,1)S(1)} %copy-done), kind=kOutput, calls=%fused_computation.62 | convolution fusion | flops 1073741824 | bytes 5242880 | tf_op jit(solution)/shard_map/dot_general | solution.py:80
  108.4 20.9 %all-gather.11.cloned.1.call-done = bf16[32,128,128]{2,1,0:T(8,128)(2,1)} async-done(((bf16[4,128,128]{2,1,0:T(8,128)(2,1)}), bf16[32,128,128]{2,1,0:T(8,128)(2,1)}) %all-gather.11.cloned.1.call-update) | async-done | bytes 1048592 | tf_op jit(solution)/shard_map/all_gather | solution.py:17
  129.2 8.5 %while.30 = (s32[]{:T(128)}, f32[4,128,128]{2,1,0:T(8,128)S(1)}, s32[]{:T(128)}, bf16[8,4,128,128]{3,2,1,0:T(8,128)(2,1)}, s32[]{:T(128)}, /*index=5*/s32[]{:T(128)}) while((s32[]{:T(128)}, f32[4,128,128]{2,1,0:T(8,128)S(1)}, s32[]{:T(128)}, bf16[8,4,128,128]{3,2,1,0:T(8,128)(2,1)}, s32[]{:T(128)}, /*index=5*/s32[]{:T(128)}) %tuple.107), condition=%wide.region_2.3_spmd.clone, body=%wide.region_1.2_spmd.clone.sunk | while | flops 262148 | bytes 655461 | solution.py:26
  137.7 2.4 multiply_reduce_fusion
  151.8 2.6 fusion.3
  154.5 12.4 %all-gather.13.cloned.1.call-done = bf16[32,128,128]{2,1,0:T(8,128)(2,1)} async-done(((bf16[4,128,128]{2,1,0:T(8,128)(2,1)}), bf16[32,128,128]{2,1,0:T(8,128)(2,1)}) %all-gather.13.cloned.1.call-update) | async-done | bytes 1048592 | tf_op jit(solution)/shard_map/all_gather | solution.py:17
  166.8 8.6 %while.31 = (s32[]{:T(128)}, f32[4,128,128]{2,1,0:T(8,128)S(1)}, s32[]{:T(128)}, bf16[8,4,128,128]{3,2,1,0:T(8,128)(2,1)}, s32[]{:T(128)}, /*index=5*/s32[]{:T(128)}, s32[]{:T(128)}, s32[]{:T(128)}) while((s32[]{:T(128)}, f32[4,128,128]{2,1,0:T(8,128)S(1)}, s32[]{:T(128)}, bf16[8,4,128,128]{3,2,1,0:T(8,128)(2,1)}, s32[]{:T(128)}, ...), condition=%wide.region_8.9_spmd.clone, body=%wide.region_7.8_spmd.clone.sunk | while | flops 262152 | bytes 655523 | solution.py:26
  179.5 7.7 %convolution_convert_fusion = bf16[512,2048]{1,0:T(8,128)(2,1)} fusion(bf16[512,1536]{0,1:T(8,128)(2,1)S(1)} %bitcast.84, bf16[2048,1536]{0,1:T(8,128)(2,1)} %bitcast.81), kind=kOutput, calls=%fused_computation.11 | convolution fusion | flops 3222274048 | bytes 9961472 | tf_op jit(solution)/shard_map/dot_general | solution.py:135
  188.3 2.6 convolution_convert_fusion.1
  191.2 8.3 %multiply_convert_fusion = bf16[2048,1536]{0,1:T(8,128)(2,1)} fusion(bf16[512,1536]{0,1:T(8,128)(2,1)} %bitcast.85, bf16[512,2048]{1,0:T(8,128)(2,1)} %all-gather.7.cloned.1.call-done, f32[2048]{0:T(1024)S(1)} %copy-done.19, f32[512]{0:T(512)S(1)} %add_rsqrt_fusion.1), kind=kOutput, calls=%fused_computation.2 | convolution fusion | flops 3231711232 | bytes 9971712 | tf_op jit(solution)/shard_map/dot_general | solution.py:122
  199.4 8.7 %copy.61 = bf16[2048,3,512]{2,0,1:T(8,128)(2,1)} copy(bf16[2048,3,512]{0,2,1:T(8,128)(2,1)} %bitcast.82) | data formatting | bytes 12582912 | tf_op jit(solution)/shard_map/convert_element_type | solution.py:128
  208.1 3.1 reduce-scatter.11.cloned.1.call-done
  213.1 44.2 %reduce-scatter.7.cloned.1.call-done = bf16[128,2048]{1,0:T(8,128)(2,1)} async-done(((bf16[512,2048]{1,0:T(8,128)(2,1)}), bf16[128,2048]{1,0:T(8,128)(2,1)}) %reduce-scatter.7.cloned.1.call-update) | async-done | bytes 524304 | tf_op jit(solution)/shard_map/reduce_scatter | solution.py:134
  258.7 44.1 %reduce-scatter.5.cloned.1.call-done = bf16[128,2048]{1,0:T(8,128)(2,1)} async-done(((bf16[512,2048]{1,0:T(8,128)(2,1)}), bf16[128,2048]{1,0:T(8,128)(2,1)}) %reduce-scatter.5.cloned.1.call-update) | async-done | bytes 524304 | tf_op jit(solution)/shard_map/reduce_scatter | solution.py:71
  302.9 2.7 fusion.15
  305.5 62.2 %reduce-scatter.9.cloned.1.call-done = bf16[256,3,512]{2,0,1:T(8,128)(2,1)} async-done(((bf16[2048,3,512]{2,0,1:T(8,128)(2,1)}), bf16[256,3,512]{2,0,1:T(8,128)(2,1)}) %reduce-scatter.9.cloned.1.call-update) | async-done | bytes 786448 | tf_op jit(solution)/shard_map/reduce_scatter | solution.py:125
  367.8 2.5 convert_element_type.139
  (99 shorter events, 47.3 us)
Async XLA Ops:
  7.2 97.3 %copy-start = (bf16[512,2048]{1,0:T(8,128)(2,1)S(1)}, bf16[512,2048]{1,0:T(8,128)(2,1)}, u32[]{:S(2)}) copy-start(bf16[512,2048]{1,0:T(8,128)(2,1)} %param.14) | copy-start | bytes 6291460
  7.2 51.1 %all-gather.7.cloned.1.call-start = ((), (), s32[]{:S(2)}) async-start(), calls=%async_computation.4 | async-start | bytes 2621440 | tf_op jit(solution)/shard_map/all_gather | solution.py:47
  7.9 96.6 %all-gather.9.cloned.1.call-start = ((), (), s32[]{:S(2)}) async-start(), calls=%async_computation.6 | async-start | bytes 2621440 | tf_op jit(solution)/shard_map/all_gather | solution.py:79
  8.7 120.6 %all-gather.11.cloned.1.call-start = ((), (), s32[]{:S(2)}) async-start(), calls=%async_computation.10 | async-start | bytes 1179648 | tf_op jit(solution)/shard_map/all_gather | solution.py:17
  8.7 51.8 %copy-start.19 = (f32[2048]{0:T(1024)S(1)}, f32[2048]{0:T(1024)}, u32[]{:S(2)}) copy-start(f32[2048]{0:T(1024)} %param.11) | copy-start | bytes 24580
  58.3 2.2 copy-start.12
  76.2 4.4 %copy-start.3 = (bf16[512,1,4,128]{0,3,2,1:T(8,128)(2,1)}, bf16[512,1,4,128]{0,3,2,1:T(8,128)(2,1)S(1)}, u32[]{:S(2)}) copy-start(bf16[512,1,4,128]{0,3,2,1:T(8,128)(2,1)S(1)} %copy.75) | copy-start | bytes 1572868
  78.5 88.3 %all-gather.13.cloned.1.call-start = ((), (), s32[]{:S(2)}) async-start(), calls=%async_computation.11 | async-start | bytes 1179648 | tf_op jit(solution)/shard_map/all_gather | solution.py:17
  78.7 2.0 copy-start.17
  108.4 29.4 %copy-start.20 = (f32[512]{0:T(512)S(1)}, f32[512]{0:T(512)}, u32[]{:S(2)}) copy-start(f32[512]{0:T(512)} %param.13) | copy-start | bytes 6148
  137.7 2.5 copy-start.10
  140.2 3.2 copy-start.18
  143.2 68.0 %reduce-scatter.11.cloned.1.call-start = ((), (), s32[]{:S(2)}) async-start(), calls=%async_computation.9 | async-start | bytes 2359296 | tf_op jit(solution)/shard_map/reduce_scatter | solution.py:93
  143.4 2.1 copy-start.5
  146.6 1.6 copy-start.2
  149.6 2.2 copy-start.21
  154.4 102.9 %reduce-scatter.7.cloned.1.call-start = ((), (), s32[]{:S(2)}) async-start(), calls=%async_computation.7 | async-start | bytes 2621440 | tf_op jit(solution)/shard_map/reduce_scatter | solution.py:134
  166.8 10.7 %copy-start.4 = (bf16[512,1,4,128]{0,3,2,1:T(8,128)(2,1)S(1)}, bf16[512,1,4,128]{0,3,2,1:T(8,128)(2,1)}, u32[]{:S(2)}) copy-start(bf16[512,1,4,128]{0,3,2,1:T(8,128)(2,1)} %copy-done.3) | copy-start | bytes 1572868
  175.4 2.2 copy-start.9
  175.4 2.8 copy-start.13
  187.3 115.6 %reduce-scatter.5.cloned.1.call-start = ((), (), s32[]{:S(2)}) async-start(), calls=%async_computation.5 | async-start | bytes 2621440 | tf_op jit(solution)/shard_map/reduce_scatter | solution.py:71
  190.9 176.9 %reduce-scatter.9.cloned.1.call-start = ((), (), s32[]{:S(2)}) async-start(), calls=%async_computation.8 | async-start | bytes 7077888 | tf_op jit(solution)/shard_map/reduce_scatter | solution.py:125
  208.1 49.3 %copy-start.8 = (bf16[128,2048]{1,0:T(8,128)(2,1)S(1)}, bf16[128,2048]{1,0:T(8,128)(2,1)}, u32[]{:S(2)}) copy-start(bf16[128,2048]{1,0:T(8,128)(2,1)} %param.10) | copy-start | bytes 1572868
  208.1 94.8 %copy-start.11 = (bf16[128,2048]{1,0:T(8,128)(2,1)S(1)}, bf16[128,2048]{1,0:T(8,128)(2,1)}, u32[]{:S(2)}) copy-start(bf16[128,2048]{1,0:T(8,128)(2,1)} %param.15) | copy-start | bytes 1572868
  (6 other events, 6.9 us)
Sparse Core Ops, SparseCore 0:
  9.6 48.6 all-gather.6
  59.8 44.6 all-gather.8
  107.0 22.1 all-gather.10
  143.3 23.4 all-gather.12
  170.0 41.2 reduce-scatter.10
  213.5 43.8 reduce-scatter.6
  259.6 43.1 reduce-scatter.4
  306.6 61.1 reduce-scatter.8
where the time goes:
time: 379 us; the launch traced here: 377 us
  waiting for transfers between devices  250 us (66%)
  matrix products  52 us (14%)
  local copies, waits for them, and re-layouts  33 us (9%)
  other arithmetic  26.8 us (7%)
  between operations  14.5 us (4%)
    reduce_scatter x1, waiting for transfers between devices, shards(): lax.psum_scatter((product * factor).reshape(ctx_rows * lax.axis_size('ctx...  62.2 us
    reduce_scatter x1, waiting for transfers between devices, shards(): lax.psum_scatter(lax.dot_general(rows, flat_weight, (((1,), (1,)), ((), (...  44.2 us
    reduce_scatter x1, waiting for transfers between devices, shards(): lax.psum_scatter(jnp.dot(rows, out_weight, preferred_element_type=jnp.flo...  44.1 us
    all_gather x1, waiting for transfers between devices, shards(): lax.all_gather(inputs, 'tp', axis=0, tiled=True).astype(jnp.float32)  40.7 us
    all_gather x2, waiting for transfers between devices, carried_in(): everything = lax.all_gather(array.astype(jnp.bfloat16), axis)  33.2 us
    all_gather x1, waiting for transfers between devices, shards(): cotangent = lax.all_gather(out_cotangent, 'tp', axis=0, tiled=True)  20.7 us
    unnamed x47, local copies, waits for them, and re-layouts  17.5 us
    select_n x16, other arithmetic, hop(): return jnp.where(reached, new, before)  16.7 us
  transfers between devices with their start and end apart: 8, of which 8 were waited for; matrix products, arithmetic and copies ran while one was open for 24% of the time, Pallas kernels for 0%

commit v1 on v0

v1 whole, which is shorter than its diff:
```python
import functools
import math

import jax
import jax.numpy as jnp
from jax import lax
from jax.experimental import pallas as pl
from jax.experimental.pallas import tpu as pltpu
from jax.sharding import PartitionSpec as P

DH = 128
EPSILON = 1e-05
MESH = pl.DeviceIdType.MESH
F32 = jnp.float32
BF16 = jnp.bfloat16
VMEM_LIMIT = 60 * 1024 * 1024
NN = (((1,), (0,)), ((), ()))
NT = (((1,), (1,)), ((), ()))
TN = (((0,), (0,)), ((), ()))


def dot(a, b, dims=NN):
    return lax.dot_general(a, b, dims, preferred_element_type=F32)


def row_scale(rows):
    return lax.rsqrt(jnp.mean(rows * rows, axis=-1, keepdims=True) + EPSILON)


def split(value):
    high = value.astype(BF16)
    return high, (value - high.astype(F32)).astype(BF16)


def line_barrier(ctx, me, n, others):
    barrier = pltpu.get_barrier_semaphore()

    @pl.when(me > 0)
    def _():
        pl.semaphore_signal(barrier, inc=1, device_id=(ctx, me - 1), device_id_type=MESH)

    @pl.when(me < n - 1)
    def _():
        pl.semaphore_signal(barrier, inc=1, device_id=(ctx, me + 1), device_id_type=MESH)

    for other in others:
        pl.semaphore_signal(barrier, inc=1, device_id=(other, me), device_id_type=MESH)
    inner = jnp.logical_and(me > 0, me < n - 1)

    @pl.when(inner)
    def _():
        pl.semaphore_wait(barrier, 2 + len(others))

    @pl.when(jnp.logical_not(inner))
    def _():
        pl.semaphore_wait(barrier, 1 + len(others))


class LineGather:
    def __init__(self, ctx, me, n, own, held, send, recv):
        self.ctx, self.me, self.n = ctx, me, n
        self.own, self.held, self.send, self.recv = own, held, send, recv

    def copy(self, source, origin, up):
        target = self.me + 1 if up else self.me - 1
        return pltpu.make_async_remote_copy(
            src_ref=source,
            dst_ref=self.held.at[origin],
            send_sem=self.send.at[1 if up else 0, origin],
            recv_sem=self.recv.at[origin],
            device_id=(self.ctx, target),
            device_id_type=MESH,
        )

    def start(self):
        @pl.when(self.me < self.n - 1)
        def _():
            self.copy(self.own, self.me, True).start()

        @pl.when(self.me > 0)
        def _():
            self.copy(self.own, self.me, False).start()

    def step(self, d):
        below, above = self.me - d, self.me + d

        @pl.when(below >= 0)
        def _():
            self.copy(self.held.at[below], below, True).wait_recv()

            @pl.when(self.me < self.n - 1)
            def _():
                self.copy(self.held.at[below], below, True).start()

        @pl.when(above < self.n)
        def _():
            self.copy(self.held.at[above], above, False).wait_recv()

            @pl.when(self.me > 0)
            def _():
                self.copy(self.held.at[above], above, False).start()

    def finish(self):
        for origin in range(self.n):

            @pl.when(jnp.logical_and(origin <= self.me, self.me < self.n - 1))
            def _():
                self.copy(self.held.at[origin], origin, True).wait_send()

            @pl.when(jnp.logical_and(origin >= self.me, self.me > 0))
            def _():
                self.copy(self.held.at[origin], origin, False).wait_send()


class LineScatter:
    def __init__(self, ctx, me, n, partial, total, out, up_in, down_in, send, recv):
        self.ctx, self.me, self.n = ctx, me, n
        self.partial, self.total, self.out = partial, total, out
        self.arrived = (down_in, up_in)
        self.send, self.recv = send, recv

    def copy(self, t, up):
        target = self.me + 1 if up else self.me - 1
        side = 1 if up else 0
        return pltpu.make_async_remote_copy(
            src_ref=self.out.at[t],
            dst_ref=self.arrived[side].at[t],
            send_sem=self.send.at[t],
            recv_sem=self.recv.at[side, t],
            device_id=(self.ctx, target),
            device_id_type=MESH,
        )

    def add(self, t, up):
        self.copy(t, up).wait_recv()
        self.total[...] += self.arrived[1 if up else 0][t].astype(F32)

    def step(self, s):
        me, n = self.me, self.n

        @pl.when(s >= me)
        def _():
            t = n - 1 - s + me
            self.partial(t, self.total)

            @pl.when(me > 0)
            def _():
                self.add(t, True)

            self.out[t] = self.total[...].astype(BF16)
            self.copy(t, True).start()

        @pl.when(s >= n - 1 - me)
        def _():
            t = s - (n - 1 - me)
            self.partial(t, self.total)

            @pl.when(me < n - 1)
            def _():
                self.add(t, False)

            self.out[t] = self.total[...].astype(BF16)
            self.copy(t, False).start()

    def finish(self):
        me, n = self.me, self.n
        self.partial(me, self.total)

        @pl.when(me > 0)
        def _():
            self.add(me, True)

        @pl.when(me < n - 1)
        def _():
            self.add(me, False)

        for t in range(n):

            @pl.when(t != me)
            def _():
                self.copy(t, True).wait_send()


def project_kernel(n, x_ref, gain_ref, w_ref, normed_ref, proj_ref, held, send, recv):
    ctx, me = lax.axis_index("ctx"), lax.axis_index("tp")
    rows = x_ref.shape[0]
    line_barrier(ctx, me, n, [])
    gather = LineGather(ctx, me, n, x_ref, held, send, recv)
    gather.start()

    def compute(source, origin):
        at = pl.ds(pl.multiple_of(origin * rows, rows), rows)
        piece = source[...].astype(F32)
        normed_ref[at, :] = (piece * row_scale(piece) * gain_ref[...]).astype(BF16)

        @pl.loop(0, w_ref.shape[1] // 512)
        def _(tile):
            columns = pl.ds(pl.multiple_of(tile * 512, 512), 512)
            proj_ref[at, columns] = dot(normed_ref[at, :], w_ref[:, columns]).astype(BF16)

    compute(x_ref, me)

    @pl.loop(1, n)
    def _(d):
        gather.step(d)

        @pl.when(me - d >= 0)
        def _():
            compute(held.at[me - d], me - d)

        @pl.when(me + d < n)
        def _():
            compute(held.at[me + d], me + d)

    gather.finish()


class StateSum:
    def __init__(self, ctx, me, chips, later, local, mine, pair, chip_sum, arrived, sems):
        self.chip, self.core = ctx // 2, lax.rem(ctx, 2)
        self.sibling = ctx + 1 - 2 * self.core
        self.me, self.chips, self.later = me, chips, later
        self.local, self.mine, self.pair = local, mine, pair
        self.chip_sum, self.arrived, self.sems = chip_sum, arrived, sems

    def pair_copy(self):
        return pltpu.make_async_remote_copy(
            src_ref=self.mine,
            dst_ref=self.pair,
            send_sem=self.sems.at[0, 0],
            recv_sem=self.sems.at[1, 0],
            device_id=(self.sibling, self.me),
            device_id_type=MESH,
        )

    def chip_copy(self, target, origin):
        return pltpu.make_async_remote_copy(
            src_ref=self.chip_sum,
            dst_ref=self.arrived.at[origin],
            send_sem=self.sems.at[0, target + 1],
            recv_sem=self.sems.at[1, origin + 1],
            device_id=(2 * target + self.core, self.me),
            device_id_type=MESH,
        )

    def wanted(self, source, target):
        return source > target if self.later else source < target

    def start(self):
        self.mine[...] = self.local[...].astype(BF16)
        self.pair_copy().start()

    def spread(self):
        self.pair_copy().wait()
        self.chip_sum[...] = (self.local[...] + self.pair[...].astype(F32)).astype(BF16)
        for other in range(self.chips):

            @pl.when(self.wanted(self.chip, other))
            def _():
                self.chip_copy(other, self.chip).start()

    def collect(self):
        near = self.core == (0 if self.later else 1)
        self.local[...] = jnp.where(near, self.pair[...].astype(F32), 0.0)
        for other in range(self.chips):

            @pl.when(self.wanted(other, self.chip))
            def _():
                self.chip_copy(other, other).wait_recv()
                self.local[...] += self.arrived[other].astype(F32)

            @pl.when(self.wanted(self.chip, other))
            def _():
                self.chip_copy(other, self.chip).wait_send()


def attend_kernel(
    n, chips, ctx_size,
    proj_ref, x_ref, cot_ref, wo_ref, gain_ref,
    outputs_ref, gproj_ref, mixed_ref, cots_ref,
    held, gsend, grecv,
    total, out, up_in, down_in, ssend, srecv,
    scores, attended, gatt, gkey,
    local_f, mine_f, pair_f, sum_f, arrived_f, sems_f,
    local_b, mine_b, pair_b, sum_b, arrived_b, sems_b,
):
    ctx, me = lax.axis_index("ctx"), lax.axis_index("tp")
    rows = x_ref.shape[0]
    block, width = mixed_ref.shape
    heads = width // DH
    chip, core = ctx // 2, lax.rem(ctx, 2)
    others = [ctx + 1 - 2 * core]
    others += [2 * lax.rem(chip + j, chips) + core for j in range(1, chips)]
    line_barrier(ctx, me, n, others)
    gather = LineGather(ctx, me, n, cot_ref, held, gsend, grecv)
    gather.start()
    forward = StateSum(ctx, me, chips, False, local_f, mine_f, pair_f, sum_f, arrived_f, sems_f)
    backward = StateSum(ctx, me, chips, True, local_b, mine_b, pair_b, sum_b, arrived_b, sems_b)

    def cols(h, part=0):
        return pl.ds(pl.multiple_of(part * width + h * DH, DH), DH)

    def head_rows(h):
        return pl.ds(pl.multiple_of(h * DH, DH), DH)

    def causal(value):
        down = lax.broadcasted_iota(jnp.int32, (block, block), 0)
        across = lax.broadcasted_iota(jnp.int32, (block, block), 1)
        return jnp.where(down >= across, value, 0.0).astype(BF16)

    @pl.loop(0, heads)
    def _(h):
        local_f[head_rows(h), :] = dot(proj_ref[:, cols(h, 1)], proj_ref[:, cols(h, 2)], TN)

    forward.start()

    @pl.loop(0, heads)
    def _(h):
        scores[h] = causal(dot(proj_ref[:, cols(h)], proj_ref[:, cols(h, 1)], NT))

    forward.spread()

    @pl.loop(0, heads)
    def _(h):
        attended[:, cols(h)] = dot(scores[h], proj_ref[:, cols(h, 2)])

    gather.step(1)
    forward.collect()

    @pl.loop(0, heads)
    def _(h):
        high, low = split(local_f[head_rows(h), :])
        query = proj_ref[:, cols(h)]
        value = attended[:, cols(h)] + dot(query, high) + dot(query, low)
        attended[:, cols(h)] = value
        mixed_ref[:, cols(h)] = (value * row_scale(value) * gain_ref[:, cols(h)]).astype(BF16)

    def partial(t, into):
        at = pl.ds(pl.multiple_of(t * rows, rows), rows)

        @pl.loop(0, wo_ref.shape[1] // 512)
        def _(tile):
            columns = pl.ds(pl.multiple_of(tile * 512, 512), 512)
            into[:, columns] = dot(mixed_ref[at, :], wo_ref[:, columns])

    scatter = LineScatter(ctx, me, n, partial, total, out, up_in, down_in, ssend, srecv)
    scatter.step(0)
    for d in range(2, n):
        gather.step(d)
        if d < n - 1:
            scatter.step(d - 1)

    def grad_rows(origin, source):
        at = pl.ds(pl.multiple_of(origin * rows, rows), rows)
        cots_ref[at, :] = source[...]
        weighted = dot(source[...], wo_ref[...], NT) * gain_ref[...]
        for h in range(heads):
            here = slice(h * DH, (h + 1) * DH)
            value = attended[at, here]
            scale = row_scale(value)
            part = weighted[:, here]
            mean = jnp.mean(part * value, axis=-1, keepdims=True)
            gatt[at, here] = (scale * part - scale * scale * scale * value * mean).astype(BF16)

    grad_rows(me, cot_ref)

    @pl.loop(1, n)
    def _(j):
        origin = lax.rem(me + j, n)
        grad_rows(origin, held.at[origin])

    @pl.loop(0, heads)
    def _(h):
        local_b[head_rows(h), :] = dot(proj_ref[:, cols(h)], gatt[:, cols(h)], TN)

    backward.start()
    for s in range(max(1, n - 2), n - 1):
        scatter.step(s)
    backward.spread()

    @pl.loop(0, heads)
    def _(h):
        query, key = proj_ref[:, cols(h)], proj_ref[:, cols(h, 1)]
        grad = gatt[:, cols(h)]
        gscores = causal(dot(grad, proj_ref[:, cols(h, 2)], NT))
        high, low = split(local_f[head_rows(h), :])
        gquery = dot(gscores, key) + dot(grad, high, NT) + dot(grad, low, NT)
        gproj_ref[:, cols(h)] = gquery.astype(BF16)
        gkey[:, cols(h)] = dot(gscores, query, TN)
        attended[:, cols(h)] = dot(scores[h], grad, TN)

    backward.collect()

    @pl.loop(0, heads)
    def _(h):
        high, low = split(local_b[head_rows(h), :])
        key, value = proj_ref[:, cols(h, 1)], proj_ref[:, cols(h, 2)]
        gk = gkey[:, cols(h)] + dot(value, high, NT) + dot(value, low, NT)
        gv = attended[:, cols(h)] + dot(key, high) + dot(key, low)
        gproj_ref[:, cols(h, 1)] = gk.astype(BF16)
        gproj_ref[:, cols(h, 2)] = gv.astype(BF16)

    scatter.finish()
    outputs_ref[...] = (x_ref[...].astype(F32) + total[...]).astype(BF16)
    gather.finish()


def reduce_kernel(
    n, chips, factor,
    normed_ref, gproj_ref, mixed_ref, cots_ref, w_ref, x_ref, cot_ref, gain_ref,
    igrad_ref, qgrad_ref, ograd_ref,
    total, out, up_in, down_in, ssend, srecv,
    kept, pair_out, pair_in, chip_out, chip_in, psend, precv, csend, crecv,
):
    ctx, me = lax.axis_index("ctx"), lax.axis_index("tp")
    rows = x_ref.shape[0]
    slab = qgrad_ref.shape[0]
    qwidth, owidth = gproj_ref.shape[1], mixed_ref.shape[1]
    chip, core = ctx // 2, lax.rem(ctx, 2)
    sibling = ctx + 1 - 2 * core
    others = [sibling]
    others += [2 * lax.rem(chip + j, chips) + core for j in range(1, chips)]
    line_barrier(ctx, me, n, others)

    def partial(t, into):
        at = pl.ds(pl.multiple_of(t * rows, rows), rows)

        @pl.loop(0, w_ref.shape[0] // 512)
        def _(tile):
            columns = pl.ds(pl.multiple_of(tile * 512, 512), 512)
            into[:, columns] = dot(gproj_ref[at, :], w_ref[columns, :], NT)

    def product(owner, store):
        step = max(slab, DH)
        first = pl.multiple_of((owner * slab) // step * step, step)
        shift = owner * slab - (owner * slab) // step * step

        def pieces(left, right, count, base):
            @pl.loop(0, count)
            def _(tile):
                columns = pl.ds(pl.multiple_of(tile * 512, 512), 512)
                value = dot(left[:, pl.ds(first, step)], right[:, columns], TN) * factor
                if step != slab:
                    half = value[:slab]
                    for k in range(1, step // slab):
                        half = jnp.where(shift == k * slab, value[k * slab : (k + 1) * slab], half)
                    value = half
                store(pl.ds(pl.multiple_of(base + tile * 512, 512), 512), value)

        pieces(normed_ref, gproj_ref, qwidth // 512, 0)
        pieces(cots_ref, mixed_ref, owidth // 512, qwidth)

    def pair_copy(p):
        return pltpu.make_async_remote_copy(
            src_ref=pair_out.at[p], dst_ref=pair_in.at[p],
            send_sem=psend.at[p], recv_sem=precv.at[p],
            device_id=(sibling, me), device_id_type=MESH,
        )

    def chip_copy(target, origin):
        return pltpu.make_async_remote_copy(
            src_ref=chip_out.at[target], dst_ref=chip_in.at[origin],
            send_sem=csend.at[target], recv_sem=crecv.at[origin],
            device_id=(2 * target + core, me), device_id_type=MESH,
        )

    scatter = LineScatter(ctx, me, n, partial, total, out, up_in, down_in, ssend, srecv)
    scatter.step(0)

    @pl.loop(1, chips + 1)
    def _(j):
        p = lax.rem(chip + j, chips)

        def store(columns, value):
            pair_out[p, :, columns] = value.astype(BF16)

        product(2 * p + 1 - core, store)
        pair_copy(p).start()

    @pl.loop(1, chips)
    def _(j):
        p = lax.rem(chip + j, chips)
        pair_copy(p).wait_recv()

        def store(columns, value):
            chip_out[p, :, columns] = (value + pair_in[p, :, columns].astype(F32)).astype(BF16)

        product(2 * p + core, store)
        chip_copy(p, chip).start()

    @pl.loop(1, n - 1)
    def _(s):
        scatter.step(s)

    pair_copy(chip).wait_recv()

    def keep(columns, value):
        kept[:, columns] = value + pair_in[chip, :, columns].astype(F32)

    product(2 * chip + core, keep)
    scatter.finish()
    piece = x_ref[...].astype(F32)
    scale = row_scale(piece)
    weighted = total[...] * gain_ref[...]
    mean = jnp.mean(weighted * piece, axis=-1, keepdims=True)
    igrad_ref[...] = (
        cot_ref[...].astype(F32) + scale * weighted - scale * scale * scale * piece * mean
    ).astype(BF16)

    @pl.loop(1, chips)
    def _(j):
        p = lax.rem(chip + chips - j, chips)
        chip_copy(p, p).wait_recv()
        kept[...] += chip_in[p].astype(F32)

    qgrad_ref[...] = kept[:, :qwidth]
    ograd_ref[...] = kept[:, qwidth:]

    @pl.loop(0, chips)
    def _(p):
        pair_copy(p).wait_send()

    @pl.loop(1, chips)
    def _(j):
        p = lax.rem(chip + j, chips)
        chip_copy(p, chip).wait_send()


def vmem(*shape, dtype=BF16):
    return pltpu.VMEM(shape, dtype)


def call(body, name, outs, scratch, collective, flops, operands):
    spec = pl.BlockSpec(memory_space=pltpu.VMEM)
    moved = sum(a.size * a.dtype.itemsize for a in list(operands) + list(outs))
    return pl.pallas_call(
        body,
        name=name,
        out_shape=outs,
        in_specs=[spec] * len(operands),
        out_specs=[spec] * len(outs),
        scratch_shapes=scratch,
        compiler_params=pltpu.CompilerParams(
            collective_id=collective, has_side_effects=True, vmem_limit_bytes=VMEM_LIMIT
        ),
        cost_estimate=pl.CostEstimate(flops=flops, bytes_accessed=moved, transcendentals=0),
    )(*operands)


def shards(inputs, norm_gain, qkv_weight, head_gain, out_weight, out_cotangent):
    rows, width = inputs.shape
    local_width = qkv_weight.shape[2]
    heads = local_width // DH
    n = lax.axis_size("tp")
    ctx_size = lax.axis_size("ctx")
    chips = ctx_size // 2
    block = rows * n
    slab = width // ctx_size
    factor = 1.0 / math.sqrt(block * ctx_size)
    flat_weight = qkv_weight.reshape(width, 3 * local_width)
    gain_row = norm_gain.reshape(1, width)
    head_row = head_gain.reshape(1, local_width)
    dma = pltpu.SemaphoreType.DMA
    shape = jax.ShapeDtypeStruct

    normed, projected = call(
        functools.partial(project_kernel, n),
        "project",
        [shape((block, width), BF16), shape((block, 3 * local_width), BF16)],
        [vmem(n, rows, width), dma((2, n)), dma((n,))],
        0,
        2 * block * width * 3 * local_width,
        (inputs, gain_row, flat_weight),
    )
    line_scratch = [
        vmem(rows, width, dtype=F32),
        vmem(n, rows, width),
        vmem(n, rows, width),
        vmem(n, rows, width),
        dma((n,)),
        dma((2, n)),
    ]
    state_scratch = [
        vmem(heads * DH, DH, dtype=F32),
        vmem(heads * DH, DH),
        vmem(heads * DH, DH),
        vmem(heads * DH, DH),
        vmem(chips, heads * DH, DH),
        dma((2, chips + 1)),
    ]
    outputs, grad_proj, mixed, cotangents = call(
        functools.partial(attend_kernel, n, chips, ctx_size),
        "attend",
        [
            shape((rows, width), BF16),
            shape((block, 3 * local_width), BF16),
            shape((block, local_width), BF16),
            shape((block, width), BF16),
        ],
        [vmem(n, rows, width), dma((2, n)), dma((n,))]
        + line_scratch
        + [
            vmem(heads, block, block),
            vmem(block, local_width, dtype=F32),
            vmem(block, local_width),
            vmem(block, local_width, dtype=F32),
        ]
        + state_scratch
        + state_scratch,
        1,
        4 * block * width * local_width + 14 * block * block * local_width,
        (projected, inputs, out_cotangent, out_weight, head_row),
    )
    both = 4 * local_width
    input_grad, qkv_grad, out_grad_t = call(
        functools.partial(reduce_kernel, n, chips, factor),
        "reduce",
        [
            shape((rows, width), BF16),
            shape((slab, 3 * local_width), F32),
            shape((slab, local_width), F32),
        ],
        line_scratch
        + [
            vmem(slab, both, dtype=F32),
            vmem(chips, slab, both),
            vmem(chips, slab, both),
            vmem(chips, slab, both),
            vmem(chips, slab, both),
            dma((chips,)),
            dma((chips,)),
            dma((chips,)),
            dma((chips,)),
        ],
        2,
        14 * block * width * local_width,
        (normed, grad_proj, mixed, cotangents, flat_weight, inputs, out_cotangent, gain_row),
    )
    return (outputs, input_grad, qkv_grad.reshape(slab, 3, local_width), out_grad_t)


def solution(mesh):
    in_specs = (
        P(("ctx", "tp"), None),
        P(),
        P(None, None, "tp"),
        P("tp"),
        P("tp", None),
        P(("ctx", "tp"), None),
    )
    out_specs = (
        P(("ctx", "tp"), None),
        P(("ctx", "tp"), None),
        P("ctx", None, "tp"),
        P("ctx", "tp"),
    )
    return jax.shard_map(shards, mesh=mesh, in_specs=in_specs, out_specs=out_specs, check_vma=False)
```

time: 379 us -> 195 us (0.51)
  waiting for transfers between devices: 250 us -> 0 us
  Pallas kernels: 0 us -> 171 us
  matrix products: 52 us -> 0 us
  other arithmetic: 26.8 us -> 0 us
  between operations: 14.5 us -> 0.69 us
  local copies, waits for them, and re-layouts: 33 us -> 23.3 us
    pallas_call x0 -> x3, Pallas kernels: none -> 171 us  [call(): pl.pallas_call(body, name=name, out_shape=outs, in_specs=[spec] * len(ope...]
    reduce_scatter x4 -> x0, waiting for transfers between devices: 154 us -> none  [the longest x1 62.2 us: shards(): lax.psum_scatter((product * factor).reshape(ctx_rows * lax.axis_size('ctx...]
    all_gather x4 -> x0, waiting for transfers between devices: 94.6 us -> none  [the longest x1 40.7 us: shards(): lax.all_gather(inputs, 'tp', axis=0, tiled=True).astype(jnp.float32)]
    dot_general x18 -> x0, matrix products: 52 us -> none  [the longest x1 8.26 us: shards(): lax.dot_general(columns, grad_proj, (((0,), (0,)), ((), ())), preferred_e...]
    select_n x16 -> x0, other arithmetic: 16.7 us -> none  [hop(): return jnp.where(reached, new, before)]
    convert_element_type x1 -> x0, local copies, waits for them, and re-layouts: 8.65 us -> none  [shards(): qkv_grad = lax.psum_scatter((product * factor).reshape(ctx_rows * lax.axi...]
    convert_element_type x3 -> x0, other arithmetic: 6.31 us -> none  [the longest x1 2.66 us: shards(): input_grad = (out_cotangent.astype(jnp.float32) + scale_in * weighted_in...]
    reshape x1, local copies, waits for them, and re-layouts: 3.93 us -> 8.61 us  [shards(): flat_weight = qkv_weight.reshape(width, 3 * local_width)]
  transfers between devices with their start and end apart: 8 -> 0, of which waited for: 8 -> 0; matrix products, arithmetic and copies ran while one was open for 24% -> 0% of each run, Pallas kernels for 0% -> 0%
where the time goes in v1:
time: 195 us
  Pallas kernels  171 us (88%)
  local copies, waits for them, and re-layouts  23.3 us (12%)
    pallas_call x3, Pallas kernels, call(): pl.pallas_call(body, name=name, out_shape=outs, in_specs=[spec] * len(ope...  171 us
    unnamed x11, local copies, waits for them, and re-layouts  12.9 us
    reshape x1, local copies, waits for them, and re-layouts, shards(): flat_weight = qkv_weight.reshape(width, 3 * local_width)  8.61 us

profile of v1, /device:TPU:0, one launch (start us, length us, event | category | flops | bytes accessed | tf_op | source)
XLA Modules:
  0.0 194.8 jit_solution(11525058329753638396)
XLA Ops:
  0.6 8.9 %copy.12 = bf16[2048,3,512]{0,2,1:T(8,128)(2,1)} copy(bf16[2048,3,512]{2,0,1:T(8,128)(2,1)} %param.8) | data formatting | bytes 12582912 | tf_op args[2]
  9.5 8.6 %copy.13.w_ref = bf16[2048,1536]{1,0:T(8,128)(2,1)} copy(bf16[2048,1536]{0,1:T(8,128)(2,1)} %bitcast.4) | data formatting | bytes 12582912 | tf_op jit(solution)/shard_map/reshape | solution.py:560
  18.1 46.7 %project.1 = (bf16[512,2048]{1,0:T(8,128)(2,1)}, bf16[512,1536]{1,0:T(8,128)(2,1)}) custom-call(bf16[128,2048]{1,0:T(8,128)(2,1)} %x_ref.5, f32[1,2048]{1,0:T(1,128)} %bitcast.6, bf16[2048,1536]{1,0:T(8,128)(2,1)} %copy.13.w_ref), custom_call_target="tpu_custom_call" | custom-call | flops 3221225472 | bytes 10493952 | tf_op jit(solution)/shard_map/project/pallas_call | solution.py:536
  64.8 57.8 %attend.1 = (bf16[128,2048]{1,0:T(8,128)(2,1)}, bf16[512,1536]{1,0:T(8,128)(2,1)}, bf16[512,512]{1,0:T(8,128)(2,1)}, bf16[512,2048]{1,0:T(8,128)(2,1)}) custom-call(bf16[512,1536]{1,0:T(8,128)(2,1)} %get-tuple-element.13.proj_ref, bf16[128,2048]{1,0:T(8,128)(2,1)} %x_ref.5, bf16[128,2048]{1,0:T(8,128)(2,1)} %cot_ref.3, bf16[512,2048]{1,0:T(8,128)(2,1)} %wo_ref.1, ...), custom_call_target="tpu_custom_call" | custom-call | flops 4026531840 | bytes 9439232 | tf_op jit(solution)/shard_map/attend/pallas_call | solution.py:536
  122.6 66.3 %reduce.1 = (bf16[128,2048]{1,0:T(8,128)(2,1)}, f32[256,1536]{1,0:T(8,128)}, f32[256,512]{1,0:T(8,128)}) custom-call(bf16[512,2048]{1,0:T(8,128)(2,1)} %get-tuple-element.15.normed_ref, bf16[512,1536]{1,0:T(8,128)(2,1)} %get-tuple-element.16.gproj_ref, bf16[512,512]{1,0:T(8,128)(2,1)} %get-tuple-element.17.mixed_ref, ...), custom_call_target="tpu_custom_call" | custom-call | flops 7516192768 | bytes 16261120 | tf_op jit(solution)/shard_map/reduce/pallas_call | solution.py:536
  188.9 1.9 copy.15
  190.8 0.0 copy-start
  190.8 0.0 copy-start.2
  190.8 0.0 copy-start.1
  190.8 1.6 copy.16
  192.4 0.0 copy-done
  192.4 0.8 copy.20
  193.2 0.0 copy-done.2
  193.2 0.8 copy.21
  194.0 0.0 copy-done.1
  194.0 0.8 copy.22
Async XLA Ops:
  190.8 1.6 copy-start
  190.8 2.4 %copy-start.2 = (bf16[128,2048]{1,0:T(8,128)(2,1)S(1)}, bf16[128,2048]{1,0:T(8,128)(2,1)}, u32[]{:S(2)}) copy-start(bf16[128,2048]{1,0:T(8,128)(2,1)} %get-tuple-element.35) | copy-start | bytes 1572868
  190.8 3.2 %copy-start.1 = (f32[256,512]{1,0:T(8,128)S(1)}, f32[256,512]{1,0:T(8,128)}, u32[]{:S(2)}) copy-start(f32[256,512]{1,0:T(8,128)} %get-tuple-element.37) | copy-start | bytes 1572868

commit v2 on v1

v2 whole, which is shorter than its diff:
```python
import functools
import math

import jax
import jax.numpy as jnp
from jax import lax
from jax.experimental import pallas as pl
from jax.experimental.pallas import tpu as pltpu
from jax.sharding import PartitionSpec as P

DH = 128
EPSILON = 1e-05
MESH = pl.DeviceIdType.MESH
F32 = jnp.float32
BF16 = jnp.bfloat16
VMEM_LIMIT = 63 * 1024 * 1024
NN = (((1,), (0,)), ((), ()))
NT = (((1,), (1,)), ((), ()))
TN = (((0,), (0,)), ((), ()))


def dot(a, b, dims=NN):
    return lax.dot_general(a, b, dims, preferred_element_type=F32)


def row_scale(rows):
    return lax.rsqrt(jnp.mean(rows * rows, axis=-1, keepdims=True) + EPSILON)


def split(value):
    high = value.astype(BF16)
    return high, (value - high.astype(F32)).astype(BF16)


def line_barrier(ctx, me, n, others):
    barrier = pltpu.get_barrier_semaphore()

    @pl.when(me > 0)
    def _():
        pl.semaphore_signal(barrier, inc=1, device_id=(ctx, me - 1), device_id_type=MESH)

    @pl.when(me < n - 1)
    def _():
        pl.semaphore_signal(barrier, inc=1, device_id=(ctx, me + 1), device_id_type=MESH)

    for other in others:
        pl.semaphore_signal(barrier, inc=1, device_id=(other, me), device_id_type=MESH)
    inner = jnp.logical_and(me > 0, me < n - 1)

    @pl.when(inner)
    def _():
        pl.semaphore_wait(barrier, 2 + len(others))

    @pl.when(jnp.logical_not(inner))
    def _():
        pl.semaphore_wait(barrier, 1 + len(others))


class LineGather:
    def __init__(self, ctx, me, n, own, held, send, recv):
        self.ctx, self.me, self.n = ctx, me, n
        self.own, self.held, self.send, self.recv = own, held, send, recv

    def at(self, origin):
        rows = self.own.shape[0]
        return self.held.at[pl.ds(pl.multiple_of(origin * rows, rows), rows), :]

    def copy(self, source, origin, up):
        target = self.me + 1 if up else self.me - 1
        return pltpu.make_async_remote_copy(
            src_ref=source,
            dst_ref=self.at(origin),
            send_sem=self.send.at[1 if up else 0, origin],
            recv_sem=self.recv.at[origin],
            device_id=(self.ctx, target),
            device_id_type=MESH,
        )

    def start_up(self):
        @pl.when(self.me < self.n - 1)
        def _():
            self.copy(self.own, self.me, True).start()

    def start_down(self):
        @pl.when(self.me > 0)
        def _():
            self.copy(self.own, self.me, False).start()

    def step(self, d):
        below, above = self.me - d, self.me + d

        @pl.when(below >= 0)
        def _():
            self.copy(self.at(below), below, True).wait_recv()

            @pl.when(self.me < self.n - 1)
            def _():
                self.copy(self.at(below), below, True).start()

        @pl.when(above < self.n)
        def _():
            self.copy(self.at(above), above, False).wait_recv()

            @pl.when(self.me > 0)
            def _():
                self.copy(self.at(above), above, False).start()

    def finish(self):
        for origin in range(self.n):

            @pl.when(jnp.logical_and(origin <= self.me, self.me < self.n - 1))
            def _():
                self.copy(self.at(origin), origin, True).wait_send()

            @pl.when(jnp.logical_and(origin >= self.me, self.me > 0))
            def _():
                self.copy(self.at(origin), origin, False).wait_send()


class LineScatter:
    def __init__(self, ctx, me, n, partial, total, out, up_in, down_in, send, recv):
        self.ctx, self.me, self.n = ctx, me, n
        self.partial, self.total, self.out = partial, total, out
        self.arrived = (down_in, up_in)
        self.send, self.recv = send, recv

    def copy(self, t, up):
        target = self.me + 1 if up else self.me - 1
        side = 1 if up else 0
        return pltpu.make_async_remote_copy(
            src_ref=self.out.at[t],
            dst_ref=self.arrived[side].at[t],
            send_sem=self.send.at[t],
            recv_sem=self.recv.at[side, t],
            device_id=(self.ctx, target),
            device_id_type=MESH,
        )

    def add(self, t, up):
        self.copy(t, up).wait_recv()
        self.total[...] += self.arrived[1 if up else 0][t].astype(F32)

    def step(self, s):
        me, n = self.me, self.n

        @pl.when(s >= me)
        def _():
            t = n - 1 - s + me
            self.partial(t, self.total)

            @pl.when(me > 0)
            def _():
                self.add(t, True)

            self.out[t] = self.total[...].astype(BF16)
            self.copy(t, True).start()

        @pl.when(s >= n - 1 - me)
        def _():
            t = s - (n - 1 - me)
            self.partial(t, self.total)

            @pl.when(me < n - 1)
            def _():
                self.add(t, False)

            self.out[t] = self.total[...].astype(BF16)
            self.copy(t, False).start()

    def finish(self):
        me, n = self.me, self.n
        self.partial(me, self.total)

        @pl.when(me > 0)
        def _():
            self.add(me, True)

        @pl.when(me < n - 1)
        def _():
            self.add(me, False)

        for t in range(n):

            @pl.when(t != me)
            def _():
                self.copy(t, True).wait_send()


class StateSum:
    def __init__(self, ctx, me, chips, later, local, mine, pair, chip_sum, arrived, sems):
        self.chip, self.core = ctx // 2, lax.rem(ctx, 2)
        self.sibling = ctx + 1 - 2 * self.core
        self.me, self.chips, self.later = me, chips, later
        self.local, self.mine, self.pair = local, mine, pair
        self.chip_sum, self.arrived, self.sems = chip_sum, arrived, sems

    def pair_copy(self):
        return pltpu.make_async_remote_copy(
            src_ref=self.mine,
            dst_ref=self.pair,
            send_sem=self.sems.at[0, 0],
            recv_sem=self.sems.at[1, 0],
            device_id=(self.sibling, self.me),
            device_id_type=MESH,
        )

    def chip_copy(self, target, origin):
        return pltpu.make_async_remote_copy(
            src_ref=self.chip_sum,
            dst_ref=self.arrived.at[origin],
            send_sem=self.sems.at[0, target + 1],
            recv_sem=self.sems.at[1, origin + 1],
            device_id=(2 * target + self.core, self.me),
            device_id_type=MESH,
        )

    def wanted(self, source, target):
        return source > target if self.later else source < target

    def start(self):
        self.mine[...] = self.local[...].astype(BF16)
        self.pair_copy().start()

    def spread(self):
        self.pair_copy().wait()
        self.chip_sum[...] = (self.local[...] + self.pair[...].astype(F32)).astype(BF16)
        for other in range(self.chips):

            @pl.when(self.wanted(self.chip, other))
            def _():
                self.chip_copy(other, self.chip).start()

    def collect(self):
        near = self.core == (0 if self.later else 1)
        self.local[...] = jnp.where(near, self.pair[...].astype(F32), 0.0)
        for other in range(self.chips):

            @pl.when(self.wanted(other, self.chip))
            def _():
                self.chip_copy(other, other).wait_recv()
                self.local[...] += self.arrived[other].astype(F32)

            @pl.when(self.wanted(self.chip, other))
            def _():
                self.chip_copy(other, self.chip).wait_send()


class SlabReduce:
    def __init__(self, ctx, me, chips, factor, left, right, kept, bufs, sems):
        self.chip, self.core = ctx // 2, lax.rem(ctx, 2)
        self.sibling = ctx + 1 - 2 * self.core
        self.me, self.chips, self.factor = me, chips, factor
        self.left, self.right, self.kept = left, right, kept
        self.pair_out, self.pair_in, self.chip_out, self.chip_in = bufs
        self.sems = sems

    def product(self, owner, store):
        slab = self.kept.shape[0]
        step = max(slab, DH)
        first = pl.multiple_of((owner * slab) // step * step, step)
        shift = owner * slab - (owner * slab) // step * step

        @pl.loop(0, self.right.shape[1] // 512)
        def _(tile):
            columns = pl.ds(pl.multiple_of(tile * 512, 512), 512)
            value = dot(self.left[:, pl.ds(first, step)], self.right[:, columns], TN)
            value = value * self.factor
            if step != slab:
                part = value[:slab]
                for k in range(1, step // slab):
                    part = jnp.where(shift == k * slab, value[k * slab : (k + 1) * slab], part)
                value = part
            store(columns, value)

    def pair_copy(self, p):
        return pltpu.make_async_remote_copy(
            src_ref=self.pair_out.at[p], dst_ref=self.pair_in.at[p],
            send_sem=self.sems.at[0, p], recv_sem=self.sems.at[1, p],
            device_id=(self.sibling, self.me), device_id_type=MESH,
        )

    def chip_copy(self, target, origin):
        return pltpu.make_async_remote_copy(
            src_ref=self.chip_out.at[target], dst_ref=self.chip_in.at[origin],
            send_sem=self.sems.at[2, target], recv_sem=self.sems.at[3, origin],
            device_id=(2 * target + self.core, self.me), device_id_type=MESH,
        )

    def run(self, between=None):
        chips, chip, core = self.chips, self.chip, self.core

        @pl.loop(1, chips + 1)
        def _(j):
            p = lax.rem(chip + j, chips)

            def store(columns, value):
                self.pair_out[p, :, columns] = value.astype(BF16)

            self.product(2 * p + 1 - core, store)
            self.pair_copy(p).start()

            @pl.when(j > 1)
            def _():
                q = lax.rem(chip + j - 1, chips)
                self.pair_copy(q).wait_recv()

                def store(columns, value):
                    value = value + self.pair_in[q, :, columns].astype(F32)
                    self.chip_out[q, :, columns] = value.astype(BF16)

                self.product(2 * q + core, store)
                self.chip_copy(q, chip).start()

            if between is not None:
                between(j)

        self.pair_copy(chip).wait_recv()

        def keep(columns, value):
            self.kept[:, columns] = value + self.pair_in[chip, :, columns].astype(F32)

        self.product(2 * chip + core, keep)

    def collect(self):
        chips, chip = self.chips, self.chip

        @pl.loop(1, chips)
        def _(j):
            p = lax.rem(chip + chips - j, chips)
            self.chip_copy(p, p).wait_recv()
            self.kept[...] += self.chip_in[p].astype(F32)

    def finish(self):
        chips, chip = self.chips, self.chip

        @pl.loop(0, chips)
        def _(p):
            self.pair_copy(p).wait_send()

        @pl.loop(1, chips)
        def _(j):
            p = lax.rem(chip + j, chips)
            self.chip_copy(p, chip).wait_send()


def block_kernel(
    n, chips, factor,
    x_ref, cot_ref, in_gain_ref, gain_ref, w_hbm, wo_hbm,
    outputs_ref, igrad_ref, qgrad_ref, ograd_ref,
    w_ref, wo_ref, load,
    normed_ref, proj_ref, mixed_ref, gproj_ref,
    held_x, xsend, xrecv,
    held_c, csend, crecv,
    total,
    out_a, up_a, down_a, asend, arecv,
    out_g, up_g, down_g, gsend, grecv,
    scores, attended, gatt, gkey,
    local_f, mine_f, pair_f, sum_f, arrived_f, sems_f,
    local_b, mine_b, pair_b, sum_b, arrived_b, sems_b,
    kept_q, q0, q1, q2, q3, qsems,
    kept_o, o0, o1, o2, o3, osems,
):
    ctx, me = lax.axis_index("ctx"), lax.axis_index("tp")
    rows = x_ref.shape[0]
    block, width = mixed_ref.shape
    heads = width // DH
    chip, core = ctx // 2, lax.rem(ctx, 2)
    w_load = pltpu.make_async_copy(w_hbm, w_ref, load.at[0])
    wo_load = pltpu.make_async_copy(wo_hbm, wo_ref, load.at[1])
    w_load.start()
    wo_load.start()
    others = [ctx + 1 - 2 * core]
    others += [2 * lax.rem(chip + j, chips) + core for j in range(1, chips)]
    line_barrier(ctx, me, n, others)
    gather_x = LineGather(ctx, me, n, x_ref, held_x, xsend, xrecv)
    gather_c = LineGather(ctx, me, n, cot_ref, held_c, csend, crecv)
    forward = StateSum(ctx, me, chips, False, local_f, mine_f, pair_f, sum_f, arrived_f, sems_f)
    backward = StateSum(ctx, me, chips, True, local_b, mine_b, pair_b, sum_b, arrived_b, sems_b)
    reduce_o = SlabReduce(
        ctx, me, chips, factor, held_c, mixed_ref, kept_o, (o0, o1, o2, o3), osems
    )
    reduce_q = SlabReduce(
        ctx, me, chips, factor, normed_ref, gproj_ref, kept_q, (q0, q1, q2, q3), qsems
    )

    def row_at(origin):
        return pl.ds(pl.multiple_of(origin * rows, rows), rows)

    def cols(h, part=0):
        return pl.ds(pl.multiple_of(part * width + h * DH, DH), DH)

    def head_rows(h):
        return pl.ds(pl.multiple_of(h * DH, DH), DH)

    def causal(value):
        down = lax.broadcasted_iota(jnp.int32, (block, block), 0)
        across = lax.broadcasted_iota(jnp.int32, (block, block), 1)
        return jnp.where(down >= across, value, 0.0).astype(BF16)

    def cotangent_turn(d):
        @pl.when(me == d)
        def _():
            gather_c.start_up()

        @pl.when(me == n - 1 - d)
        def _():
            gather_c.start_down()

    def project(source, origin):
        at = row_at(origin)
        piece = source[...].astype(F32)
        normed_ref[at, :] = (piece * row_scale(piece) * in_gain_ref[...]).astype(BF16)
        for part in range(3):
            here = slice(part * width, (part + 1) * width)
            proj_ref[at, here] = dot(normed_ref[at, :], w_ref[part]).astype(BF16)

    gather_x.start_up()
    gather_x.start_down()
    cotangent_turn(0)
    held_c[row_at(me), :] = cot_ref[...]
    w_load.wait()
    project(x_ref, me)

    @pl.loop(1, n)
    def _(d):
        gather_x.step(d)
        cotangent_turn(d)

        @pl.when(me - d >= 0)
        def _():
            project(gather_x.at(me - d), me - d)

        @pl.when(me + d < n)
        def _():
            project(gather_x.at(me + d), me + d)

    @pl.loop(0, heads)
    def _(h):
        local_f[head_rows(h), :] = dot(proj_ref[:, cols(h, 1)], proj_ref[:, cols(h, 2)], TN)

    forward.start()

    @pl.loop(0, heads)
    def _(h):
        scores[h] = causal(dot(proj_ref[:, cols(h)], proj_ref[:, cols(h, 1)], NT))

    forward.spread()
    gather_c.step(1)

    @pl.loop(0, heads)
    def _(h):
        attended[:, cols(h)] = dot(scores[h], proj_ref[:, cols(h, 2)])

    forward.collect()

    @pl.loop(0, heads)
    def _(h):
        high, low = split(local_f[head_rows(h), :])
        query = proj_ref[:, cols(h)]
        value = attended[:, cols(h)] + dot(query, high) + dot(query, low)
        attended[:, cols(h)] = value
        mixed_ref[:, cols(h)] = (value * row_scale(value) * gain_ref[:, cols(h)]).astype(BF16)

    wo_load.wait()

    def out_partial(t, into):
        @pl.loop(0, wo_ref.shape[1] // 512)
        def _(tile):
            columns = pl.ds(pl.multiple_of(tile * 512, 512), 512)
            into[:, columns] = dot(mixed_ref[row_at(t), :], wo_ref[:, columns])

    scatter = LineScatter(ctx, me, n, out_partial, total, out_a, up_a, down_a, asend, arecv)
    scatter.step(0)

    def grad_rows(origin):
        at = row_at(origin)
        weighted = dot(held_c[at, :], wo_ref[...], NT) * gain_ref[...]
        for h in range(heads):
            here = slice(h * DH, (h + 1) * DH)
            value = attended[at, here]
            scale = row_scale(value)
            part = weighted[:, here]
            mean = jnp.mean(part * value, axis=-1, keepdims=True)
            gatt[at, here] = (scale * part - scale * scale * scale * value * mean).astype(BF16)

    def grad_pair(d):
        @pl.when(me - d >= 0)
        def _():
            grad_rows(me - d)

        @pl.when(me + d < n)
        def _():
            grad_rows(me + d)

    gather_c.step(2)
    grad_rows(me)

    @pl.loop(1, n - 1)
    def _(d):
        grad_pair(d)

    scatter.step(1)
    for d in range(3, n):
        gather_c.step(d)
        grad_pair(d)

    @pl.loop(0, heads)
    def _(h):
        local_b[head_rows(h), :] = dot(proj_ref[:, cols(h)], gatt[:, cols(h)], TN)

    backward.start()

    @pl.loop(0, heads)
    def _(h):
        query, key = proj_ref[:, cols(h)], proj_ref[:, cols(h, 1)]
        grad = gatt[:, cols(h)]
        gscores = causal(dot(grad, proj_ref[:, cols(h, 2)], NT))
        high, low = split(local_f[head_rows(h), :])
        gquery = dot(gscores, key) + dot(grad, high, NT) + dot(grad, low, NT)
        gproj_ref[:, cols(h)] = gquery.astype(BF16)
        gkey[:, cols(h)] = dot(gscores, query, TN)

        @pl.when(h == 0)
        def _():
            backward.spread()

    @pl.loop(0, heads)
    def _(h):
        attended[:, cols(h)] = dot(scores[h], gatt[:, cols(h)], TN)

    for s in range(2, n - 1):
        scatter.step(s)
    reduce_o.run()
    backward.collect()

    @pl.loop(0, heads)
    def _(h):
        high, low = split(local_b[head_rows(h), :])
        key, value = proj_ref[:, cols(h, 1)], proj_ref[:, cols(h, 2)]
        gk = gkey[:, cols(h)] + dot(value, high, NT) + dot(value, low, NT)
        gv = attended[:, cols(h)] + dot(key, high) + dot(key, low)
        gproj_ref[:, cols(h, 1)] = gk.astype(BF16)
        gproj_ref[:, cols(h, 2)] = gv.astype(BF16)

    scatter.finish()
    outputs_ref[...] = (x_ref[...].astype(F32) + total[...]).astype(BF16)

    def in_partial(t, into):
        at = row_at(t)

        @pl.loop(0, w_ref.shape[1] // 512)
        def _(tile):
            columns = pl.ds(pl.multiple_of(tile * 512, 512), 512)
            value = dot(gproj_ref[at, :width], w_ref[0, columns, :], NT)
            for part in range(1, 3):
                here = slice(part * width, (part + 1) * width)
                value += dot(gproj_ref[at, here], w_ref[part, columns, :], NT)
            into[:, columns] = value

    back = LineScatter(ctx, me, n, in_partial, total, out_g, up_g, down_g, gsend, grecv)
    back.step(0)

    def between(j):
        @pl.when(j == chips)
        def _():
            back.step(1)

    reduce_q.run(between)
    for s in range(2, n - 1):
        back.step(s)
    reduce_o.collect()
    ograd_ref[...] = kept_o[...]
    back.finish()
    piece = x_ref[...].astype(F32)
    scale = row_scale(piece)
    weighted = total[...] * in_gain_ref[...]
    mean = jnp.mean(weighted * piece, axis=-1, keepdims=True)
    igrad_ref[...] = (
        cot_ref[...].astype(F32) + scale * weighted - scale * scale * scale * piece * mean
    ).astype(BF16)
    reduce_q.collect()
    for part in range(3):
        qgrad_ref[part] = kept_q[:, part * width : (part + 1) * width]
    gather_x.finish()
    gather_c.finish()
    reduce_o.finish()
    reduce_q.finish()


def vmem(*shape, dtype=BF16):
    return pltpu.VMEM(shape, dtype)


def shards(inputs, norm_gain, qkv_weight, head_gain, out_weight, out_cotangent):
    rows, width = inputs.shape
    local_width = qkv_weight.shape[2]
    heads = local_width // DH
    n = lax.axis_size("tp")
    ctx_size = lax.axis_size("ctx")
    chips = ctx_size // 2
    block = rows * n
    slab = width // ctx_size
    factor = 1.0 / math.sqrt(block * ctx_size)
    dma = pltpu.SemaphoreType.DMA
    shape = jax.ShapeDtypeStruct
    gather = [vmem(block, width), dma((2, n)), dma((n,))]
    line = [vmem(n, rows, width)] * 3 + [dma((n,)), dma((2, n))]
    state = [
        vmem(heads * DH, DH, dtype=F32),
        vmem(heads * DH, DH),
        vmem(heads * DH, DH),
        vmem(heads * DH, DH),
        vmem(chips, heads * DH, DH),
        dma((2, chips + 1)),
    ]

    def slabs(columns):
        return [vmem(slab, columns, dtype=F32)] + [vmem(chips, slab, columns)] * 4 + [
            dma((4, chips))
        ]

    scratch = (
        [vmem(3, width, local_width), vmem(local_width, width), dma((2,))]
        + [vmem(block, width), vmem(block, 3 * local_width)]
        + [vmem(block, local_width), vmem(block, 3 * local_width)]
        + gather
        + gather
        + [vmem(rows, width, dtype=F32)]
        + line
        + line
        + [vmem(heads, block, block), vmem(block, local_width, dtype=F32)]
        + [vmem(block, local_width), vmem(block, local_width, dtype=F32)]
        + state
        + state
        + slabs(3 * local_width)
        + slabs(local_width)
    )
    held = pl.BlockSpec(memory_space=pltpu.VMEM)
    anywhere = pl.BlockSpec(memory_space=pl.ANY)
    outputs, input_grad, qkv_grad, out_grad_t = pl.pallas_call(
        functools.partial(block_kernel, n, chips, factor),
        name="block",
        out_shape=[
            shape((rows, width), BF16),
            shape((rows, width), BF16),
            shape((3, slab, local_width), F32),
            shape((slab, local_width), F32),
        ],
        in_specs=[held] * 4 + [anywhere] * 2,
        out_specs=[held] * 4,
        scratch_shapes=scratch,
        compiler_params=pltpu.CompilerParams(
            collective_id=0, has_side_effects=True, vmem_limit_bytes=VMEM_LIMIT
        ),
    )(
        inputs,
        out_cotangent,
        norm_gain.reshape(1, width),
        head_gain.reshape(1, local_width),
        qkv_weight.transpose(1, 0, 2),
        out_weight,
    )
    return (outputs, input_grad, qkv_grad.transpose(1, 0, 2), out_grad_t)


def solution(mesh):
    in_specs = (
        P(("ctx", "tp"), None),
        P(),
        P(None, None, "tp"),
        P("tp"),
        P("tp", None),
        P(("ctx", "tp"), None),
    )
    out_specs = (
        P(("ctx", "tp"), None),
        P(("ctx", "tp"), None),
        P("ctx", None, "tp"),
        P("ctx", "tp"),
    )
    return jax.shard_map(shards, mesh=mesh, in_specs=in_specs, out_specs=out_specs, check_vma=False)
```

time: 195 us -> 152 us (0.78)
  Pallas kernels: 171 us -> 145 us
  local copies, waits for them, and re-layouts: 23.3 us -> 5.88 us
    pallas_call x3 -> x1, Pallas kernels: 171 us -> 145 us  [shards(): pl.pallas_call(functools.partial(block_kernel, n, chips, factor), name='b...]
    reshape x1 -> x0, local copies, waits for them, and re-layouts: 8.61 us -> none  [shards(): flat_weight = qkv_weight.reshape(width, 3 * local_width)]
    unnamed x11 -> x8, local copies, waits for them, and re-layouts: 12.9 us -> 5.88 us
where the time goes in v2:
time: 152 us
  Pallas kernels  145 us (95%)
  local copies, waits for them, and re-layouts  5.88 us (4%)
    pallas_call x1, Pallas kernels, shards(): pl.pallas_call(functools.partial(block_kernel, n, chips, factor), name='b...  145 us
    unnamed x8, local copies, waits for them, and re-layouts  5.88 us

profile of v2, /device:TPU:0, one launch (start us, length us, event | category | flops | bytes accessed | tf_op | source)
XLA Modules:
  0.0 151.7 jit_solution(10957581839006570817)
XLA Ops:
  0.6 145.1 %block.1 = (bf16[128,2048]{1,0:T(8,128)(2,1)}, bf16[128,2048]{1,0:T(8,128)(2,1)}, f32[3,256,512]{2,1,0:T(8,128)}, f32[256,512]{1,0:T(8,128)}) custom-call(bf16[128,2048]{1,0:T(8,128)(2,1)} %x_ref.1, bf16[128,2048]{1,0:T(8,128)(2,1)} %cot_ref.1, f32[1,2048]{1,0:T(1,128)} %bitcast.6, f32[1,512]{1,0:T(1,128)} %bitcast.7, bf16[3,2048,512]{2,1,0:T(8,128)(2,1)} %bitcast.4, ...), custom_call_target="tpu_custom_call" | custom-call | tf_op jit(solution)/shard_map/block/pallas_call | solution.py:640
  145.8 0.0 copy-start
  145.8 2.0 %copy.14 = bf16[128,2048]{1,0:T(8,128)(2,1)} copy(bf16[128,2048]{1,0:T(8,128)(2,1)} %get-tuple-element.16) | data formatting | bytes 1048576
  147.8 0.0 copy-start.1
  147.8 1.9 %copy.15 = bf16[128,2048]{1,0:T(8,128)(2,1)} copy(bf16[128,2048]{1,0:T(8,128)(2,1)} %get-tuple-element.17) | data formatting | bytes 1048576
  149.7 0.0 copy-done
  149.7 1.1 copy.16
  150.9 0.0 copy-done.1
  150.9 0.8 copy.17
Async XLA Ops:
  145.8 4.0 %copy-start = (f32[3,256,512]{2,1,0:T(8,128)S(1)}, f32[3,256,512]{2,1,0:T(8,128)}, u32[]{:S(2)}) copy-start(f32[3,256,512]{2,1,0:T(8,128)} %get-tuple-element.10) | copy-start | bytes 4718596
  147.8 3.1 %copy-start.1 = (f32[256,512]{1,0:T(8,128)S(1)}, f32[256,512]{1,0:T(8,128)}, u32[]{:S(2)}) copy-start(f32[256,512]{1,0:T(8,128)} %get-tuple-element.19) | copy-start | bytes 1572868

commit v3 on v2

--- a/solution.py
+++ b/solution.py
@@ -246,11 +246,11 @@
 
 
 class SlabReduce:
-    def __init__(self, ctx, me, chips, factor, left, right, kept, bufs, sems):
+    def __init__(self, ctx, me, chips, factor, left, right, base, kept, bufs, sems):
         self.chip, self.core = ctx // 2, lax.rem(ctx, 2)
         self.sibling = ctx + 1 - 2 * self.core
         self.me, self.chips, self.factor = me, chips, factor
-        self.left, self.right, self.kept = left, right, kept
+        self.left, self.right, self.base, self.kept = left, right, base, kept
         self.pair_out, self.pair_in, self.chip_out, self.chip_in = bufs
         self.sems = sems
 
@@ -260,10 +260,11 @@
         first = pl.multiple_of((owner * slab) // step * step, step)
         shift = owner * slab - (owner * slab) // step * step
 
-        @pl.loop(0, self.right.shape[1] // 512)
+        @pl.loop(0, self.kept.shape[1] // 512)
         def _(tile):
             columns = pl.ds(pl.multiple_of(tile * 512, 512), 512)
-            value = dot(self.left[:, pl.ds(first, step)], self.right[:, columns], TN)
+            source = pl.ds(pl.multiple_of(self.base + tile * 512, 512), 512)
+            value = dot(self.left[:, pl.ds(first, step)], self.right[:, source], TN)
             value = value * self.factor
             if step != slab:
                 part = value[:slab]
@@ -286,40 +287,30 @@
             device_id=(2 * target + self.core, self.me), device_id_type=MESH,
         )
 
-    def run(self, between=None):
-        chips, chip, core = self.chips, self.chip, self.core
-
-        @pl.loop(1, chips + 1)
-        def _(j):
-            p = lax.rem(chip + j, chips)
-
-            def store(columns, value):
-                self.pair_out[p, :, columns] = value.astype(BF16)
-
-            self.product(2 * p + 1 - core, store)
-            self.pair_copy(p).start()
-
-            @pl.when(j > 1)
-            def _():
-                q = lax.rem(chip + j - 1, chips)
-                self.pair_copy(q).wait_recv()
-
-                def store(columns, value):
-                    value = value + self.pair_in[q, :, columns].astype(F32)
-                    self.chip_out[q, :, columns] = value.astype(BF16)
-
-                self.product(2 * q + core, store)
-                self.chip_copy(q, chip).start()
-
-            if between is not None:
-                between(j)
-
-        self.pair_copy(chip).wait_recv()
+    def to_pair(self, p):
+        def store(columns, value):
+            self.pair_out[p, :, columns] = value.astype(BF16)
+
+        self.product(2 * p + 1 - self.core, store)
+        self.pair_copy(p).start()
+
+    def to_chip(self, q):
+        self.pair_copy(q).wait_recv()
+
+        def store(columns, value):
+            value = value + self.pair_in[q, :, columns].astype(F32)
+            self.chip_out[q, :, columns] = value.astype(BF16)
+
+        self.product(2 * q + self.core, store)
+        self.chip_copy(q, self.chip).start()
+
+    def keep_own(self):
+        self.pair_copy(self.chip).wait_recv()
 
         def keep(columns, value):
-            self.kept[:, columns] = value + self.pair_in[chip, :, columns].astype(F32)
-
-        self.product(2 * chip + core, keep)
+            self.kept[:, columns] = value + self.pair_in[self.chip, :, columns].astype(F32)
+
+        self.product(2 * self.chip + self.core, keep)
 
     def collect(self):
         chips, chip = self.chips, self.chip
@@ -341,6 +332,23 @@
         def _(j):
             p = lax.rem(chip + j, chips)
             self.chip_copy(p, chip).wait_send()
+
+
+def run_slabs(parts, between=None):
+    chips, chip = parts[0].chips, parts[0].chip
+
+    @pl.loop(1, chips + 1)
+    def _(j):
+        for part in parts:
+            part.to_pair(lax.rem(chip + j, chips))
+
+        @pl.when(j > 1)
+        def _():
+            for part in parts:
+                part.to_chip(lax.rem(chip + j - 1, chips))
+
+        if between is not None:
+            between(j)
 
 
 def block_kernel(
@@ -358,6 +366,7 @@
     local_f, mine_f, pair_f, sum_f, arrived_f, sems_f,
     local_b, mine_b, pair_b, sum_b, arrived_b, sems_b,
     kept_q, q0, q1, q2, q3, qsems,
+    kept_k, k0, k1, k2, k3, ksems,
     kept_o, o0, o1, o2, o3, osems,
 ):
     ctx, me = lax.axis_index("ctx"), lax.axis_index("tp")
@@ -377,10 +386,13 @@
     forward = StateSum(ctx, me, chips, False, local_f, mine_f, pair_f, sum_f, arrived_f, sems_f)
     backward = StateSum(ctx, me, chips, True, local_b, mine_b, pair_b, sum_b, arrived_b, sems_b)
     reduce_o = SlabReduce(
-        ctx, me, chips, factor, held_c, mixed_ref, kept_o, (o0, o1, o2, o3), osems
+        ctx, me, chips, factor, held_c, mixed_ref, 0, kept_o, (o0, o1, o2, o3), osems
     )
     reduce_q = SlabReduce(
-        ctx, me, chips, factor, normed_ref, gproj_ref, kept_q, (q0, q1, q2, q3), qsems
+        ctx, me, chips, factor, normed_ref, gproj_ref, 0, kept_q, (q0, q1, q2, q3), qsems
+    )
+    reduce_k = SlabReduce(
+        ctx, me, chips, factor, normed_ref, gproj_ref, width, kept_k, (k0, k1, k2, k3), ksems
     )
 
     def row_at(origin):
@@ -530,7 +542,7 @@
 
     for s in range(2, n - 1):
         scatter.step(s)
-    reduce_o.run()
+    run_slabs([reduce_o, reduce_q])
     backward.collect()
 
     @pl.loop(0, heads)
@@ -541,9 +553,6 @@
         gv = attended[:, cols(h)] + dot(key, high) + dot(key, low)
         gproj_ref[:, cols(h, 1)] = gk.astype(BF16)
         gproj_ref[:, cols(h, 2)] = gv.astype(BF16)
-
-    scatter.finish()
-    outputs_ref[...] = (x_ref[...].astype(F32) + total[...]).astype(BF16)
 
     def in_partial(t, into):
         at = row_at(t)
@@ -565,11 +574,18 @@
         def _():
             back.step(1)
 
-    reduce_q.run(between)
+    run_slabs([reduce_k], between)
+    reduce_k.keep_own()
+    scatter.finish()
+    outputs_ref[...] = (x_ref[...].astype(F32) + total[...]).astype(BF16)
     for s in range(2, n - 1):
         back.step(s)
+    reduce_o.keep_own()
+    reduce_q.keep_own()
     reduce_o.collect()
     ograd_ref[...] = kept_o[...]
+    reduce_q.collect()
+    qgrad_ref[0] = kept_q[...]
     back.finish()
     piece = x_ref[...].astype(F32)
     scale = row_scale(piece)
@@ -578,13 +594,14 @@
     igrad_ref[...] = (
         cot_ref[...].astype(F32) + scale * weighted - scale * scale * scale * piece * mean
     ).astype(BF16)
-    reduce_q.collect()
-    for part in range(3):
-        qgrad_ref[part] = kept_q[:, part * width : (part + 1) * width]
+    reduce_k.collect()
+    for part in range(2):
+        qgrad_ref[part + 1] = kept_k[:, part * width : (part + 1) * width]
     gather_x.finish()
     gather_c.finish()
     reduce_o.finish()
     reduce_q.finish()
+    reduce_k.finish()
 
 
 def vmem(*shape, dtype=BF16):
@@ -632,7 +649,8 @@
         + [vmem(block, local_width), vmem(block, local_width, dtype=F32)]
         + state
         + state
-        + slabs(3 * local_width)
+        + slabs(local_width)
+        + slabs(2 * local_width)
         + slabs(local_width)
     )
     held = pl.BlockSpec(memory_space=pltpu.VMEM)

time: 152 us -> 146 us (0.961)
  Pallas kernels: 145 us -> 139 us
    pallas_call x1, Pallas kernels: 145 us -> 139 us  [shards(): pl.pallas_call(functools.partial(block_kernel, n, chips, factor), name='b...]
where the time goes in v3:
time: 146 us
  Pallas kernels  139 us (95%)
  local copies, waits for them, and re-layouts  5.88 us (4%)
    pallas_call x1, Pallas kernels, shards(): pl.pallas_call(functools.partial(block_kernel, n, chips, factor), name='b...  139 us
    unnamed x8, local copies, waits for them, and re-layouts  5.88 us

profile of v3, /device:TPU:0, one launch (start us, length us, event | category | flops | bytes accessed | tf_op | source)
XLA Modules:
  0.0 145.7 jit_solution(12733932097443996857)
XLA Ops:
  0.6 139.1 %block.1 = (bf16[128,2048]{1,0:T(8,128)(2,1)}, bf16[128,2048]{1,0:T(8,128)(2,1)}, f32[3,256,512]{2,1,0:T(8,128)}, f32[256,512]{1,0:T(8,128)}) custom-call(bf16[128,2048]{1,0:T(8,128)(2,1)} %x_ref.1, bf16[128,2048]{1,0:T(8,128)(2,1)} %cot_ref.1, f32[1,2048]{1,0:T(1,128)} %bitcast.6, f32[1,512]{1,0:T(1,128)} %bitcast.7, bf16[3,2048,512]{2,1,0:T(8,128)(2,1)} %bitcast.4, ...), custom_call_target="tpu_custom_call" | custom-call | tf_op jit(solution)/shard_map/block/pallas_call | solution.py:658
  139.8 0.0 copy-start
  139.8 2.0 %copy.14 = bf16[128,2048]{1,0:T(8,128)(2,1)} copy(bf16[128,2048]{1,0:T(8,128)(2,1)} %get-tuple-element.16) | data formatting | bytes 1048576
  141.8 0.0 copy-start.1
  141.8 1.9 %copy.15 = bf16[128,2048]{1,0:T(8,128)(2,1)} copy(bf16[128,2048]{1,0:T(8,128)(2,1)} %get-tuple-element.17) | data formatting | bytes 1048576
  143.7 0.0 copy-done
  143.7 1.1 copy.16
  144.9 0.0 copy-done.1
  144.9 0.8 copy.17
Async XLA Ops:
  139.8 4.0 %copy-start = (f32[3,256,512]{2,1,0:T(8,128)S(1)}, f32[3,256,512]{2,1,0:T(8,128)}, u32[]{:S(2)}) copy-start(f32[3,256,512]{2,1,0:T(8,128)} %get-tuple-element.10) | copy-start | bytes 4718596
  141.8 3.1 %copy-start.1 = (f32[256,512]{1,0:T(8,128)S(1)}, f32[256,512]{1,0:T(8,128)}, u32[]{:S(2)}) copy-start(f32[256,512]{1,0:T(8,128)} %get-tuple-element.19) | copy-start | bytes 1572868

commit v4 on v3

--- a/solution.py
+++ b/solution.py
@@ -312,10 +312,10 @@
 
         self.product(2 * self.chip + self.core, keep)
 
-    def collect(self):
+    def collect(self, first=1, last=None):
         chips, chip = self.chips, self.chip
 
-        @pl.loop(1, chips)
+        @pl.loop(first, chips if last is None else last)
         def _(j):
             p = lax.rem(chip + chips - j, chips)
             self.chip_copy(p, p).wait_recv()
@@ -577,7 +577,7 @@
     run_slabs([reduce_k], between)
     reduce_k.keep_own()
     scatter.finish()
-    outputs_ref[...] = (x_ref[...].astype(F32) + total[...]).astype(BF16)
+    outputs_ref[...] = total[...]
     for s in range(2, n - 1):
         back.step(s)
     reduce_o.keep_own()
@@ -586,6 +586,7 @@
     ograd_ref[...] = kept_o[...]
     reduce_q.collect()
     qgrad_ref[0] = kept_q[...]
+    reduce_k.collect(1, chips - 1)
     back.finish()
     piece = x_ref[...].astype(F32)
     scale = row_scale(piece)
@@ -594,7 +595,7 @@
     igrad_ref[...] = (
         cot_ref[...].astype(F32) + scale * weighted - scale * scale * scale * piece * mean
     ).astype(BF16)
-    reduce_k.collect()
+    reduce_k.collect(chips - 1)
     for part in range(2):
         qgrad_ref[part + 1] = kept_k[:, part * width : (part + 1) * width]
     gather_x.finish()
@@ -655,11 +656,11 @@
     )
     held = pl.BlockSpec(memory_space=pltpu.VMEM)
     anywhere = pl.BlockSpec(memory_space=pl.ANY)
-    outputs, input_grad, qkv_grad, out_grad_t = pl.pallas_call(
+    summed, input_grad, qkv_grad, out_grad_t = pl.pallas_call(
         functools.partial(block_kernel, n, chips, factor),
         name="block",
         out_shape=[
-            shape((rows, width), BF16),
+            shape((rows, width), F32),
             shape((rows, width), BF16),
             shape((3, slab, local_width), F32),
             shape((slab, local_width), F32),
@@ -678,6 +679,7 @@
         qkv_weight.transpose(1, 0, 2),
         out_weight,
     )
+    outputs = (inputs.astype(F32) + summed).astype(BF16)
     return (outputs, input_grad, qkv_grad.transpose(1, 0, 2), out_grad_t)
 
 

time: 146 us -> 148 us (1.014); the launches traced: 146 us -> 146 us
  local copies, waits for them, and re-layouts: 5.88 us -> 2.75 us
  other arithmetic: 0 us -> 2.27 us
    unnamed x8 -> x11, local copies, waits for them, and re-layouts: 5.88 us -> 2.75 us
    convert_element_type x0 -> x1, other arithmetic: none -> 2.27 us  [shards(): outputs = (inputs.astype(F32) + summed).astype(BF16)]
where the time goes in v4:
time: 148 us; the launch traced here: 146 us
  Pallas kernels  140 us (95%)
  local copies, waits for them, and re-layouts  2.75 us (2%)
  other arithmetic  2.27 us (2%)
    pallas_call x1, Pallas kernels, shards(): pl.pallas_call(functools.partial(block_kernel, n, chips, factor), name='b...  140 us

profile of v4, /device:TPU:0, one launch (start us, length us, event | category | flops | bytes accessed | tf_op | source)
XLA Modules:
  0.0 145.9 jit_solution(17844716788321040960)
XLA Ops:
  0.6 0.0 copy-start
  0.6 140.2 %block.1 = (f32[128,2048]{1,0:T(8,128)}, bf16[128,2048]{1,0:T(8,128)(2,1)}, f32[3,256,512]{2,1,0:T(8,128)}, f32[256,512]{1,0:T(8,128)}) custom-call(bf16[128,2048]{1,0:T(8,128)(2,1)} %x_ref.1, bf16[128,2048]{1,0:T(8,128)(2,1)} %cot_ref.1, f32[1,2048]{1,0:T(1,128)} %bitcast.6, f32[1,512]{1,0:T(1,128)} %bitcast.7, bf16[3,2048,512]{2,1,0:T(8,128)(2,1)} %bitcast.4, ...), custom_call_target="tpu_custom_call" | custom-call | tf_op jit(solution)/shard_map/block/pallas_call | solution.py:659
  140.9 0.0 copy-start.3
  140.9 0.0 copy-start.1
  140.9 0.0 copy-done
  140.9 2.3 %add_convert_fusion = bf16[128,2048]{1,0:T(8,128)(2,1)} fusion(f32[128,2048]{1,0:T(8,128)} %get-tuple-element.8, bf16[128,2048]{1,0:T(8,128)(2,1)S(1)} %copy-done), kind=kLoop, calls=%fused_computation | loop fusion | flops 786432 | bytes 2097152 | tf_op jit(solution)/shard_map/convert_element_type | solution.py:682
  143.2 0.0 copy-done.3
  143.2 0.0 copy-start.2
  143.2 0.8 copy.13
  144.0 0.0 copy-done.1
  144.0 1.1 copy.14
  145.1 0.0 copy-done.2
  145.1 0.8 copy.15
Async XLA Ops:
  0.6 140.3 %copy-start = (bf16[128,2048]{1,0:T(8,128)(2,1)S(1)}, bf16[128,2048]{1,0:T(8,128)(2,1)}, u32[]{:S(2)}) copy-start(bf16[128,2048]{1,0:T(8,128)(2,1)} %x_ref.1) | copy-start | bytes 1572868
  140.9 2.3 %copy-start.3 = (bf16[128,2048]{1,0:T(8,128)(2,1)S(1)}, bf16[128,2048]{1,0:T(8,128)(2,1)}, u32[]{:S(2)}) copy-start(bf16[128,2048]{1,0:T(8,128)(2,1)} %get-tuple-element.17) | copy-start | bytes 1572868
  140.9 3.1 %copy-start.1 = (f32[3,256,512]{2,1,0:T(8,128)S(1)}, f32[3,256,512]{2,1,0:T(8,128)}, u32[]{:S(2)}) copy-start(f32[3,256,512]{2,1,0:T(8,128)} %get-tuple-element.10) | copy-start | bytes 4718596
  143.2 1.9 %copy-start.2 = (f32[256,512]{1,0:T(8,128)S(1)}, f32[256,512]{1,0:T(8,128)}, u32[]{:S(2)}) copy-start(f32[256,512]{1,0:T(8,128)} %get-tuple-element.19) | copy-start | bytes 1572868
